TPU v7x, 256 devices: a whole 4x4x8 slice. The times are simulated.
256 devices in a mesh: ctx: 64 (over z, x, core), rows: 4 (over y).
Axes of the slice: x: 4, y: 4, z: 8, core: 2. Of those that a mesh axis runs over, the one named last changes fastest.
Arguments:
- hidden: bfloat16 [2, 4, 8192], P(None, 'rows'), may hold values from -6 to 6
- norm_gain: bfloat16 [8192], replicated, may hold values from 0.099609375 to 1.8984375
- w_query: bfloat16 [8192, 8192], P(None, 'ctx'), may hold values from -2 to 2
- w_key: bfloat16 [8192, 1024], P(None, 'ctx'), may hold values from -2 to 2
- w_value: bfloat16 [8192, 1024], P(None, 'ctx'), may hold values from -0.0625 to 0.0625
- w_out: bfloat16 [8192, 8192], P('ctx'), may hold values from -0.0625 to 0.0625
- cache_keys: bfloat16 [4, 131072, 8, 128], P('rows', 'ctx'), may hold values from -1200 to 1200
- cache_values: bfloat16 [4, 131072, 8, 128], P('rows', 'ctx'), may hold values from -24 to 24
- lengths: int32 [4], P('rows'), may hold values from 1 to 131072, as said below
- positions: int32 [4], P('rows'), may hold values from 0 to 8191
Outputs:
- attended: bfloat16 [2, 8192, 4], P(None, 'ctx', 'rows')
Inputs may be any that keep to these rules, and one draw needn't show every extreme that they name: `lengths`: one sequence has exactly 131072 live tokens and another at most 32; slots at or past a sequence's length hold entries that must not be read.
All inputs are finite; a program needn't handle non-finite values.
Results may differ from a plain program's by a relative error of at most 0.02.
The roundings to bfloat16 on the way count: a program that leaves them out, or rounds other values in their place, can miss the bound.
Values may be sent and summed in bfloat16 or wider, within the bound.
A program may use at most 64 MiB of HBM per device.

v0:
```python
import math
import jax
import jax.numpy as jnp
from jax import lax
from jax.sharding import PartitionSpec as P

theta_base = 500000.0
epsilon = 1e-05


def in_one_piece(arrays, axis, dim, along):
    widths = [a.shape[along] for a in arrays]
    both = jnp.concatenate(arrays, axis=along)
    whole = lax.all_gather(both, axis, axis=dim, tiled=True)
    return tuple(jnp.split(whole, [sum(widths[:k]) for k in range(1, len(widths))], axis=along))


def in_one_piece_2(arrays, axis, split_dim, concat_dim, along):
    widths = [math.prod(a.shape[along:]) for a in arrays]
    both = jnp.concatenate(
        [a.reshape(*a.shape[:along], w) for a, w in zip(arrays, widths)], axis=along
    )
    whole = lax.all_to_all(both, axis, split_axis=split_dim, concat_axis=concat_dim, tiled=True)
    tiles = jnp.split(whole, [sum(widths[:k]) for k in range(1, len(widths))], axis=along)
    return tuple((b.reshape(*whole.shape[:along], *a.shape[along:]) for a, b in zip(arrays, tiles)))


def in_blocks(shard, dim, peers):
    shape = shard.shape
    tiles = shard.reshape(*shape[:dim], peers, shape[dim] // peers, *shape[dim + 1 :])
    return jnp.moveaxis(tiles, dim, 0)


def sum_at_owner(shard, axis, dim):
    tiles = in_blocks(shard, dim, lax.axis_size(axis))
    arrived = lax.all_to_all(tiles, axis, split_axis=0, concat_axis=0, tiled=True)
    return arrived.sum(axis=0)


def rotate(vectors, places):
    halfway = vectors.shape[-1] // 2
    inverse = theta_base ** (-(jnp.arange(halfway, dtype=jnp.float32) * 2.0 / vectors.shape[-1]))
    angles = places.astype(jnp.float32)[:, None, None] * inverse
    cosines = jnp.cos(angles)
    sines = jnp.sin(angles)
    leading = vectors[..., :halfway]
    trailing = vectors[..., halfway:]
    return jnp.concatenate(
        [leading * cosines - trailing * sines, trailing * cosines + leading * sines], -1
    )


def normalize(inputs, norm_gain):
    scaled = inputs * lax.rsqrt(jnp.mean(inputs * inputs, -1, keepdims=True) + epsilon)
    return (scaled * norm_gain.astype(jnp.float32)).astype(jnp.bfloat16)


def local_part(grouped, cache_keys, cache_values, live_len, block_size, limit, scale_factor):
    row_count, kv_heads, group_size, head_size = grouped.shape

    def one_block(block_index, carried):
        run_max, numer, denom = carried
        key_block = lax.dynamic_slice_in_dim(cache_keys, block_index * block_size, block_size, 1)
        value_block = lax.dynamic_slice_in_dim(
            cache_values, block_index * block_size, block_size, 1
        )
        scores = (
            jnp.einsum("rkgd,rtkd->rkgt", grouped, key_block, preferred_element_type=jnp.float32)
            * scale_factor
        )
        slots = block_index * block_size + jnp.arange(block_size)
        visible = slots[None, None, None, :] < live_len[:, None, None, None]
        scores = jnp.where(visible, scores, -1e30)
        new_max = jnp.maximum(run_max, jnp.max(scores, -1))
        shrink = jnp.exp(run_max - new_max)
        weights = jnp.where(visible, jnp.exp(scores - new_max[..., None]), 0.0)
        denom = denom * shrink + jnp.sum(weights, -1)
        numer = numer * shrink[..., None] + jnp.einsum(
            "rkgt,rtkd->rkgd",
            weights.astype(jnp.bfloat16),
            value_block,
            preferred_element_type=jnp.float32,
        )
        return (new_max, numer, denom)

    initial = (
        jnp.full((row_count, kv_heads, group_size), -1e30, jnp.float32),
        jnp.zeros((row_count, kv_heads, group_size, head_size), jnp.float32),
        jnp.zeros((row_count, kv_heads, group_size), jnp.float32),
    )
    run_max, numer, denom = lax.fori_loop(0, limit, one_block, initial)
    total_heads = kv_heads * group_size
    return (
        run_max.reshape(row_count, total_heads),
        numer.reshape(row_count, total_heads, head_size),
        denom.reshape(row_count, total_heads),
    )


def on_device(
    hidden, norm_gain, w_query, w_key, w_value, w_out, cache_keys, cache_values, lengths, positions
):
    devices = lax.axis_size("ctx")
    ctx_index = lax.axis_index("ctx")
    step_count = hidden.shape[0]
    row_count = hidden.shape[1]
    head_size = cache_keys.shape[3]
    kv_heads = cache_keys.shape[2]
    local_span = cache_keys.shape[1]
    own_heads = w_query.shape[1] // head_size
    total_heads = own_heads * devices
    group_size = total_heads // kv_heads
    scale_factor = 1.0 / math.sqrt(head_size)
    block_size = min(512, local_span)
    limit = local_span // block_size
    live_len = jnp.clip(lengths - ctx_index * local_span, 0, local_span)
    head_start = ctx_index * own_heads
    kv_index = head_start // group_size
    fresh_keys = []
    fresh_values = []
    results = []
    for step_index in range(step_count):
        layer_in = hidden[step_index].astype(jnp.float32)
        normed = normalize(layer_in, norm_gain)
        query_local = jnp.dot(normed, w_query, preferred_element_type=jnp.float32).astype(
            jnp.bfloat16
        )
        key_local = jnp.dot(normed, w_key, preferred_element_type=jnp.float32).astype(jnp.bfloat16)
        value_local = jnp.dot(normed, w_value, preferred_element_type=jnp.float32).astype(
            jnp.bfloat16
        )
        query_all, key_all, value_all = (
            lax.all_gather(query_local, "ctx", axis=1, tiled=True),
            *in_one_piece((key_local, value_local), "ctx", 1, 0),
        )
        places = positions + step_index
        queries = rotate(
            query_all.astype(jnp.float32).reshape(row_count, total_heads, head_size), places
        ).astype(jnp.bfloat16)
        new_keys = rotate(
            key_all.astype(jnp.float32).reshape(row_count, kv_heads, head_size), places
        ).astype(jnp.bfloat16)
        fresh_keys.append(new_keys)
        fresh_values.append(value_all.reshape(row_count, kv_heads, head_size))
        grouped = queries.reshape(row_count, kv_heads, group_size, head_size)
        run_max, numer, denom = local_part(
            grouped, cache_keys, cache_values, live_len, block_size, limit, scale_factor
        )
        got_max, got_num, got_den = tuple(
            (
                part.astype(jnp.float32)
                for part in in_one_piece_2(
                    (
                        run_max.astype(jnp.bfloat16),
                        numer.astype(jnp.bfloat16),
                        denom.astype(jnp.bfloat16),
                    ),
                    "ctx",
                    1,
                    1,
                    2,
                )
            )
        )
        got_max = got_max.reshape(row_count, devices, own_heads)
        got_num = got_num.reshape(row_count, devices, own_heads, head_size)
        got_den = got_den.reshape(row_count, devices, own_heads)
        own_max = jnp.max(got_max, 1)
        factors = jnp.exp(got_max - own_max[:, None, :])
        own_num = jnp.sum(got_num * factors[..., None], 1)
        own_den = jnp.sum(got_den * factors, 1)
        own_query = lax.dynamic_slice_in_dim(queries, head_start, own_heads, 1)
        stacked_keys = lax.dynamic_index_in_dim(
            jnp.stack(fresh_keys, 1), kv_index, 2, keepdims=False
        )
        stacked_values = lax.dynamic_index_in_dim(
            jnp.stack(fresh_values, 1), kv_index, 2, keepdims=False
        )
        fresh_scores = (
            jnp.einsum("rjd,rtd->rjt", own_query, stacked_keys, preferred_element_type=jnp.float32)
            * scale_factor
        )
        final_max = jnp.maximum(own_max, jnp.max(fresh_scores, -1))
        shrink = jnp.exp(own_max - final_max)
        fresh_weights = jnp.exp(fresh_scores - final_max[..., None])
        final_den = own_den * shrink + jnp.sum(fresh_weights, -1)
        final_num = own_num * shrink[..., None] + jnp.einsum(
            "rjt,rtd->rjd",
            fresh_weights.astype(jnp.bfloat16),
            stacked_values,
            preferred_element_type=jnp.float32,
        )
        head_out = (
            (final_num / final_den[..., None])
            .astype(jnp.bfloat16)
            .reshape(row_count, own_heads * head_size)
        )
        summed = sum_at_owner(
            lax.dot_general(
                w_out, head_out, (((0,), (1,)), ((), ())), preferred_element_type=jnp.float32
            ),
            "ctx",
            0,
        )
        results.append(summed.astype(jnp.bfloat16))
    return jnp.stack(results, 0)


def solution(mesh):
    in_specs = (
        P(None, "rows", None),
        P(),
        P(None, "ctx"),
        P(None, "ctx"),
        P(None, "ctx"),
        P("ctx", None),
        P("rows", "ctx", None, None),
        P("rows", "ctx", None, None),
        P("rows"),
        P("rows"),
    )
    out_specs = P(None, "ctx", "rows")
    return jax.shard_map(
        on_device, mesh=mesh, in_specs=in_specs, out_specs=out_specs, check_vma=False
    )
```

profile of v0, /device:TPU:1, one launch (start us, length us, event | category | flops | bytes accessed | tf_op | source)
XLA Modules:
  0.0 265.3 jit_solution(8186538398806153378)
XLA Ops:
  0.0 1.7 multiply_reduce_fusion.1
  3.1 0.9 convert_multiply_fusion.3
  4.0 0.7 fusion.65
  5.5 2.0 fusion.59
  7.5 44.0 %all-gather.2 = bf16[64,1,128]{2,1,0:T(2,128)(2,1)S(1)} all-gather(bf16[1,1,128]{2,1,0:T(2,128)(2,1)S(1)} %fusion.59), channel_id=2, replica_groups=mesh['ctx'=64,'rows'=4] {'ctx'}, dimensions={0}, use_global_device_ids=true | all-gather | bytes 16640 | tf_op jit(solution)/shard_map/all_gather | solution.py:133
  52.1 4.8 %copy.55 = bf16[1,2048,8,128]{3,1,2,0:T(8,128)(2,1)} copy(bf16[1,2048,8,128]{3,2,1,0:T(8,128)(2,1)} %param.20) | data formatting | bytes 8388608
  57.0 2.6 copy.56
  59.8 14.0 %while.36 = (s32[]{:T(128)}, f32[1,8,8]{2,1,0:T(8,128)S(1)}, f32[1,8,8,128]{3,2,1,0:T(8,128)S(1)}, f32[1,8,8]{2,1,0:T(8,128)S(1)}, s32[1]{0:T(128)}, /*index=5*/...) while((s32[]{:T(128)}, f32[1,8,8]{2,1,0:T(8,128)S(1)}, ...), condition=%wide.region_4.5_spmd.clone, body=%wide.region_1.4_spmd.clone.sunk | while | flops 17098120 | bytes 2578623 | solution.py:91
  59.8 1.7 fusion.143
  61.6 1.6 fusion.145
  63.1 0.2 fusion.146
  63.3 1.7 fusion.143
  65.0 1.6 fusion.145
  66.6 0.2 fusion.146
  66.8 1.7 fusion.143
  68.5 1.6 fusion.145
  70.1 0.2 fusion.146
  70.3 1.7 fusion.143
  72.0 1.6 fusion.145
  73.6 0.2 fusion.146
  74.1 0.7 copy.59
  74.8 6.4 %all-to-all-start = ((bf16[1,64,130]{2,0,1:T(2,128)(2,1)}), bf16[1,64,130]{2,0,1:T(2,128)(2,1)S(1)}, u32[]{:S(2)}, u32[]{:S(2)}) async-start(bf16[1,64,130]{2,0,1:T(2,128)(2,1)} %copy.59), calls=%async_computation | async-start | bytes 131072 | tf_op jit(solution)/shard_map/all_to_all | solution.py:23
  81.2 0.2 fusion.55
  81.4 0.2 fusion.57
  81.7 0.2 fusion.49
  81.9 0.2 fusion.51
  82.1 2.0 fusion.53
  84.1 41.3 %all-gather.3 = bf16[64,16,2]{1,2,0:T(2,128)(2,1)S(1)} all-gather(bf16[1,16,2]{1,2,0:T(2,128)(2,1)S(1)} %maximum_bitcast_fusion), channel_id=1, replica_groups=mesh['ctx'=64,'rows'=4] {'ctx'}, dimensions={0}, use_global_device_ids=true | all-gather | bytes 4160 | tf_op jit(solution)/shard_map/all_gather | solution.py:14
  125.4 0.1 reshape.834
  125.5 37.3 %all-gather.5 = bf16[64,16,2]{1,2,0:T(2,128)(2,1)S(1)} all-gather(bf16[1,16,2]{1,2,0:T(2,128)(2,1)S(1)} %maximum_bitcast_fusion.1), channel_id=1, replica_groups=mesh['ctx'=64,'rows'=4] {'ctx'}, dimensions={0}, use_global_device_ids=true | all-gather | bytes 4160 | tf_op jit(solution)/shard_map/all_gather | solution.py:14
  162.9 0.1 reshape.838
  163.2 38.0 %all-gather.4 = bf16[64,1,128]{2,1,0:T(2,128)(2,1)S(1)} all-gather(bf16[1,1,128]{2,1,0:T(2,128)(2,1)S(1)} %fusion.53), channel_id=3, replica_groups=mesh['ctx'=64,'rows'=4] {'ctx'}, dimensions={0}, use_global_device_ids=true | all-gather | bytes 16640 | tf_op jit(solution)/shard_map/all_gather | solution.py:133
  201.5 13.9 %while.37 = (s32[]{:T(128)}, f32[1,8,8]{2,1,0:T(8,128)S(1)}, f32[1,8,8,128]{3,2,1,0:T(8,128)S(1)}, f32[1,8,8]{2,1,0:T(8,128)S(1)}, s32[1]{0:T(128)}, /*index=5*/...) while((s32[]{:T(128)}, f32[1,8,8]{2,1,0:T(8,128)S(1)}, ...), condition=%wide.region_13.14_spmd.clone, body=%wide.region_10.13_spmd.clone.sunk | while | flops 17098120 | bytes 2578623 | solution.py:91
  201.5 1.7 fusion.149
  203.2 1.6 fusion.151
  204.7 0.2 fusion.152
  205.0 1.7 fusion.149
  206.7 1.6 fusion.151
  208.2 0.2 fusion.152
  208.5 1.7 fusion.149
  210.2 1.6 fusion.151
  211.7 0.2 fusion.152
  212.0 1.7 fusion.149
  213.7 1.6 fusion.151
  215.2 0.2 fusion.152
  215.7 0.8 fusion.114
  216.7 0.7 copy.65
  217.3 0.7 fusion.83
  218.7 5.7 %all-to-all-start.2 = ((bf16[1,64,130]{2,0,1:T(2,128)(2,1)}), bf16[1,64,130]{2,0,1:T(2,128)(2,1)S(1)}, u32[]{:S(2)}, u32[]{:S(2)}) async-start(bf16[1,64,130]{2,0,1:T(2,128)(2,1)} %copy.65), calls=%async_computation.2 | async-start | bytes 131072 | tf_op jit(solution)/shard_map/all_to_all | solution.py:23
  224.3 0.7 slice_reduce_fusion.1
  225.7 1.0 fusion.72
  227.4 0.2 fusion.71
  227.7 1.0 fusion.42
  228.7 5.8 %all-to-all-done.2 = bf16[1,64,130]{2,0,1:T(2,128)(2,1)S(1)} async-done(((bf16[1,64,130]{2,0,1:T(2,128)(2,1)}), bf16[1,64,130]{2,0,1:T(2,128)(2,1)S(1)}, u32[]{:S(2)}, u32[]{:S(2)}) %all-to-all-start.2) | async-done | bytes 16672 | tf_op jit(solution)/shard_map/all_to_all | solution.py:23
  234.4 4.5 %all-to-all-start.1 = ((f32[64,128,1]{1,2,0:T(1,128)}), f32[64,128,1]{1,2,0:T(1,128)S(1)}, u32[]{:S(2)}, u32[]{:S(2)}) async-start(f32[64,128,1]{1,2,0:T(1,128)} %fusion.42), calls=%async_computation.1 | async-start | bytes 65536 | tf_op jit(solution)/shard_map/all_to_all | solution.py:36
  239.0 0.7 slice_reduce_fusion
  240.9 0.6 fusion.109
  241.5 1.0 fusion.74
  243.7 0.2 fusion.73
  243.9 1.1 fusion.45
  245.0 3.3 %all-to-all-done.1 = f32[64,128,1]{1,2,0:T(1,128)S(1)} async-done(((f32[64,128,1]{1,2,0:T(1,128)}), f32[64,128,1]{1,2,0:T(1,128)S(1)}, u32[]{:S(2)}, u32[]{:S(2)}) %all-to-all-start.1) | async-done | bytes 32800 | tf_op jit(solution)/shard_map/all_to_all | solution.py:36
  248.3 7.0 %all-to-all-start.3 = ((f32[64,128,1]{1,2,0:T(1,128)}), f32[64,128,1]{1,2,0:T(1,128)S(1)}, u32[]{:S(2)}, u32[]{:S(2)}) async-start(f32[64,128,1]{1,2,0:T(1,128)} %fusion.45), calls=%async_computation.3 | async-start | bytes 65536 | tf_op jit(solution)/shard_map/all_to_all | solution.py:36
  255.4 9.3 %all-to-all-done.3 = f32[64,128,1]{1,2,0:T(1,128)S(1)} async-done(((f32[64,128,1]{1,2,0:T(1,128)}), f32[64,128,1]{1,2,0:T(1,128)S(1)}, u32[]{:S(2)}, u32[]{:S(2)}) %all-to-all-start.3) | async-done | bytes 32800 | tf_op jit(solution)/shard_map/all_to_all | solution.py:36
  264.8 0.5 copy.69
  (81 shorter events, 1.9 us)
Async XLA Ops:
  0.0 227.7 %copy-start = (bf16[128,8192]{1,0:T(8,128)(2,1)S(1)}, bf16[128,8192]{1,0:T(8,128)(2,1)}, u32[]{:S(2)}) copy-start(bf16[128,8192]{1,0:T(8,128)(2,1)} %param.19) | copy-start | bytes 6291460
  52.1 4.8 %copy-start.1 = (bf16[1,2048,8,128]{3,2,1,0:T(8,128)(2,1)S(1)}, bf16[1,2048,8,128]{3,2,1,0:T(8,128)(2,1)}, u32[]{:S(2)}) copy-start(bf16[1,2048,8,128]{3,2,1,0:T(8,128)(2,1)} %param.21) | copy-start | bytes 12582916
  59.8 21.5 %copy-start.2 = (bf16[8192,16]{0,1:T(8,128)(2,1)S(1)}, bf16[8192,16]{0,1:T(8,128)(2,1)}, u32[]{:S(2)}) copy-start(bf16[8192,16]{0,1:T(8,128)(2,1)} %param.18) | copy-start | bytes 786436
  59.8 21.7 %copy-start.3 = (bf16[8192,16]{0,1:T(8,128)(2,1)S(1)}, bf16[8192,16]{0,1:T(8,128)(2,1)}, u32[]{:S(2)}) copy-start(bf16[8192,16]{0,1:T(8,128)(2,1)} %param.17) | copy-start | bytes 786436
  74.8 143.9 %all-to-all-start = ((bf16[1,64,130]{2,0,1:T(2,128)(2,1)}), bf16[1,64,130]{2,0,1:T(2,128)(2,1)S(1)}, u32[]{:S(2)}, u32[]{:S(2)}) async-start(bf16[1,64,130]{2,0,1:T(2,128)(2,1)} %copy.59), calls=%async_computation | async-start | bytes 131072 | tf_op jit(solution)/shard_map/all_to_all | solution.py:23
  218.7 15.7 %all-to-all-start.2 = ((bf16[1,64,130]{2,0,1:T(2,128)(2,1)}), bf16[1,64,130]{2,0,1:T(2,128)(2,1)S(1)}, u32[]{:S(2)}, u32[]{:S(2)}) async-start(bf16[1,64,130]{2,0,1:T(2,128)(2,1)} %copy.65), calls=%async_computation.2 | async-start | bytes 131072 | tf_op jit(solution)/shard_map/all_to_all | solution.py:23
  234.4 13.9 %all-to-all-start.1 = ((f32[64,128,1]{1,2,0:T(1,128)}), f32[64,128,1]{1,2,0:T(1,128)S(1)}, u32[]{:S(2)}, u32[]{:S(2)}) async-start(f32[64,128,1]{1,2,0:T(1,128)} %fusion.42), calls=%async_computation.1 | async-start | bytes 65536 | tf_op jit(solution)/shard_map/all_to_all | solution.py:36
  248.3 16.4 %all-to-all-start.3 = ((f32[64,128,1]{1,2,0:T(1,128)}), f32[64,128,1]{1,2,0:T(1,128)S(1)}, u32[]{:S(2)}, u32[]{:S(2)}) async-start(f32[64,128,1]{1,2,0:T(1,128)} %fusion.45), calls=%async_computation.3 | async-start | bytes 65536 | tf_op jit(solution)/shard_map/all_to_all | solution.py:36
where the time goes:
time: 267 us; the launch traced here: 265 us
  blocking collectives  161 us (60%)
  matrix products  33.6 us (13%)
  starting transfers between devices  23.6 us (9%)
  waiting for transfers between devices  18.3 us (7%)
  other arithmetic  11.3 us (4%)
  local copies, waits for them, and re-layouts  9.95 us (4%)
  between operations  7.52 us (3%)
    all_gather x2, blocking collectives, on_device(): lax.all_gather(query_local, 'ctx', axis=1, tiled=True)  82 us
    all_gather x2, blocking collectives, in_one_piece(): whole = lax.all_gather(both, axis, axis=dim, tiled=True)  78.6 us
    dot_general x8, matrix products, one_block(): jnp.einsum('rkgd,rtkd->rkgt', grouped, key_block, preferred_element_type=...  13.5 us
    all_to_all x2, waiting for transfers between devices, sum_at_owner(): lax.all_to_all(tiles, axis, split_axis=0, concat_axis=0, tiled=True)  12.6 us
    dot_general x8, matrix products, one_block(): jnp.einsum('rkgt,rtkd->rkgd', weights.astype(jnp.bfloat16), value_block,...  12.4 us
    all_to_all x2, starting transfers between devices, in_one_piece_2(): lax.all_to_all(both, axis, split_axis=split_dim, concat_axis=concat_dim,...  12.1 us
    all_to_all x2, starting transfers between devices, sum_at_owner(): lax.all_to_all(tiles, axis, split_axis=0, concat_axis=0, tiled=True)  11.5 us
    unnamed x12, local copies, waits for them, and re-layouts  7.67 us
  transfers between devices with their start and end apart: 4, of which 3 were waited for; matrix products, arithmetic and copies ran while one was open for 10% of the time, Pallas kernels for 0%

commit v1 on v0

--- a/solution.py
+++ b/solution.py
@@ -1,11 +1,28 @@
+import functools
 import math
 import jax
 import jax.numpy as jnp
 from jax import lax
 from jax.sharding import PartitionSpec as P
+from jax.lax import axis_index, axis_size, ppermute
 
 theta_base = 500000.0
 epsilon = 1e-05
+
+
+def lift_slots(field, axis_key):
+    arr_next, lower = (axis_size(axis_key), axis_index(axis_key))
+    r1, now = (field, 1)
+    while now < arr_next:
+        right_arr = ppermute(r1, axis_key, list(map(lambda p: (p, p ^ now), range(arr_next))))
+        val = jnp.concatenate([r1, right_arr], axis=1)
+        part_now = jnp.concatenate([right_arr, r1], axis=1)
+        r1 = jnp.where(lower & now == 0, val, part_now)
+        now = 2 * now
+    return r1
+
+
+finish_units_in = functools.partial(lift_slots, axis_key="ctx")
 
 
 def in_one_piece(arrays, axis, dim, along):
@@ -130,7 +147,7 @@
             jnp.bfloat16
         )
         query_all, key_all, value_all = (
-            lax.all_gather(query_local, "ctx", axis=1, tiled=True),
+            finish_units_in(query_local),
             *in_one_piece((key_local, value_local), "ctx", 1, 0),
         )
         places = positions + step_index

time: 267 us -> 216 us (0.81)
  blocking collectives: 161 us -> 78.6 us
  starting transfers between devices: 23.6 us -> 51.1 us
  waiting for transfers between devices: 18.3 us -> 23.2 us
    all_gather x2 -> x0, blocking collectives: 82 us -> none  [on_device(): lax.all_gather(query_local, 'ctx', axis=1, tiled=True)]
    ppermute x0 -> x12, starting transfers between devices: none -> 17.4 us  [lift_slots(): ppermute(r1, axis_key, list(map(lambda p: (p, p ^ now), range(arr_next))))]
    all_to_all x2, starting transfers between devices: 12.1 us -> 22.2 us  [in_one_piece_2(): lax.all_to_all(both, axis, split_axis=split_dim, concat_axis=concat_dim,...]
    ppermute x0 -> x12, waiting for transfers between devices: none -> 4.88 us  [lift_slots(): ppermute(r1, axis_key, list(map(lambda p: (p, p ^ now), range(arr_next))))]
    unnamed x12 -> x14, local copies, waits for them, and re-layouts: 7.67 us -> 7.68 us
  transfers between devices with their start and end apart: 4 -> 16, of which waited for: 3 -> 9; matrix products, arithmetic and copies ran while one was open for 10% -> 22% of each run, Pallas kernels for 0% -> 0%
where the time goes in v1:
time: 216 us; the launch traced here: 215 us
  blocking collectives  78.6 us (36%)
  starting transfers between devices  51.1 us (24%)
  matrix products  32 us (15%)
  waiting for transfers between devices  23.2 us (11%)
  other arithmetic  11.9 us (6%)
  local copies, waits for them, and re-layouts  10 us (5%)
  between operations  7.73 us (4%)
    all_gather x2, blocking collectives, in_one_piece(): whole = lax.all_gather(both, axis, axis=dim, tiled=True)  78.6 us
    all_to_all x2, starting transfers between devices, in_one_piece_2(): lax.all_to_all(both, axis, split_axis=split_dim, concat_axis=concat_dim,...  22.2 us
    ppermute x12, starting transfers between devices, lift_slots(): ppermute(r1, axis_key, list(map(lambda p: (p, p ^ now), range(arr_next))))  17.4 us
    dot_general x8, matrix products, one_block(): jnp.einsum('rkgd,rtkd->rkgt', grouped, key_block, preferred_element_type=...  13.5 us
    all_to_all x2, waiting for transfers between devices, sum_at_owner(): lax.all_to_all(tiles, axis, split_axis=0, concat_axis=0, tiled=True)  12.6 us
    dot_general x8, matrix products, one_block(): jnp.einsum('rkgt,rtkd->rkgd', weights.astype(jnp.bfloat16), value_block,...  12.4 us
    all_to_all x2, starting transfers between devices, sum_at_owner(): lax.all_to_all(tiles, axis, split_axis=0, concat_axis=0, tiled=True)  11.5 us
    unnamed x14, local copies, waits for them, and re-layouts  7.68 us
  transfers between devices with their start and end apart: 16, of which 9 were waited for; matrix products, arithmetic and copies ran while one was open for 22% of the time, Pallas kernels for 0%

profile of v1, /device:TPU:1, one launch (start us, length us, event | category | flops | bytes accessed | tf_op | source)
XLA Modules:
  0.0 214.9 jit_solution(5077157894162417466)
XLA Ops:
  0.0 1.7 multiply_reduce_fusion.1
  3.1 1.0 convert_multiply_fusion.3
  4.1 0.7 fusion.63
  4.9 2.0 fusion.57
  6.9 3.3 %collective-permute-start = (bf16[1,128]{1,0:T(2,128)(2,1)S(1)}, bf16[1,128]{1,0:T(2,128)(2,1)S(1)}, u32[]{:S(2)}, u32[]{:S(2)}) collective-permute-start(bf16[1,128]{1,0:T(2,128)(2,1)S(1)} %bitcast.334), channel_id=1, source_target_pairs={{0,4},{4,0},{8,12},{12,8},{16,20},{20,16},{24,28},{28,24},{32,36},... | collective-permute-start | bytes 776 | tf_op jit(solution)/shard_map/ppermute | solution.py:17
  10.3 0.4 fusion.52
  11.2 0.2 fusion.56
  12.4 41.2 %all-gather = bf16[64,16,2]{1,2,0:T(2,128)(2,1)S(1)} all-gather(bf16[1,16,2]{1,2,0:T(2,128)(2,1)S(1)} %maximum_bitcast_fusion), channel_id=1, replica_groups=mesh['ctx'=64,'rows'=4] {'ctx'}, dimensions={0}, use_global_device_ids=true | all-gather | bytes 4160 | tf_op jit(solution)/shard_map/all_gather | solution.py:31
  53.7 37.3 %all-gather.1 = bf16[64,16,2]{1,2,0:T(2,128)(2,1)S(1)} all-gather(bf16[1,16,2]{1,2,0:T(2,128)(2,1)S(1)} %maximum_bitcast_fusion.1), channel_id=1, replica_groups=mesh['ctx'=64,'rows'=4] {'ctx'}, dimensions={0}, use_global_device_ids=true | all-gather | bytes 4160 | tf_op jit(solution)/shard_map/all_gather | solution.py:31
  91.8 4.8 %copy.55 = bf16[1,2048,8,128]{3,1,2,0:T(8,128)(2,1)} copy(bf16[1,2048,8,128]{3,2,1,0:T(8,128)(2,1)} %param.20) | data formatting | bytes 8388608
  96.6 2.6 %copy.56 = bf16[1,2048,8,128]{3,1,2,0:T(8,128)(2,1)} copy(bf16[1,2048,8,128]{3,2,1,0:T(8,128)(2,1)S(1)} %copy-done.2) | data formatting | bytes 8388608
  99.7 1.0 collective-permute-start.1
  100.7 0.6 collective-permute-start.7
  101.4 0.8 collective-permute-done.1
  102.2 1.8 collective-permute-start.2
  104.0 1.4 collective-permute-start.8
  105.5 0.8 collective-permute-done.2
  106.5 1.8 collective-permute-done.8
  108.4 0.3 collective-permute-start.9
  108.9 1.6 collective-permute-start.4
  110.5 0.4 collective-permute-done.9
  110.9 1.6 collective-permute-start.10
  112.7 3.1 %collective-permute-start.5 = (bf16[1,4096]{1,0:T(2,128)(2,1)S(1)}, bf16[1,4096]{1,0:T(2,128)(2,1)S(1)}, u32[]{:S(2)}, u32[]{:S(2)}) collective-permute-start(bf16[1,4096]{1,0:T(2,128)(2,1)S(1)} %broadcast_select_fusion.1), channel_id=1, source_target_pairs={{0,128},{4,132},{8,136},{12,140},{16,144},{20,148},{24,152},{28,15... | collective-permute-start | bytes 24584 | tf_op jit(solution)/shard_map/ppermute | solution.py:17
  115.8 2.4 %collective-permute-start.11 = (bf16[1,4096]{1,0:T(2,128)(2,1)S(1)}, bf16[1,4096]{1,0:T(2,128)(2,1)S(1)}, u32[]{:S(2)}, u32[]{:S(2)}) collective-permute-start(bf16[1,4096]{1,0:T(2,128)(2,1)S(1)} %broadcast_select_fusion), channel_id=1, source_target_pairs={{0,128},{4,132},{8,136},{12,140},{16,144},{20,148},{24,152},{28,15... | collective-permute-start | bytes 24584 | tf_op jit(solution)/shard_map/ppermute | solution.py:17
  118.3 0.9 collective-permute-done.5
  119.5 13.9 %while.36 = (s32[]{:T(128)}, f32[1,8,8]{2,1,0:T(8,128)S(1)}, f32[1,8,8,128]{3,2,1,0:T(8,128)S(1)}, f32[1,8,8]{2,1,0:T(8,128)S(1)}, s32[1]{0:T(128)}, /*index=5*/...) while((s32[]{:T(128)}, f32[1,8,8]{2,1,0:T(8,128)S(1)}, ...), condition=%wide.region_4.5_spmd.clone, body=%wide.region_1.4_spmd.clone.sunk | while | flops 17098120 | bytes 2578623 | solution.py:108
  119.5 1.7 fusion.145
  121.2 1.6 fusion.147
  123.0 1.7 fusion.145
  124.7 1.6 fusion.147
  126.5 1.7 fusion.145
  128.2 1.6 fusion.147
  130.0 1.7 fusion.145
  131.7 1.6 fusion.147
  133.7 0.7 copy.59
  134.4 11.9 %all-to-all-start = ((bf16[1,64,130]{2,0,1:T(2,128)(2,1)}), bf16[1,64,130]{2,0,1:T(2,128)(2,1)S(1)}, u32[]{:S(2)}, u32[]{:S(2)}) async-start(bf16[1,64,130]{2,0,1:T(2,128)(2,1)} %copy.59), calls=%async_computation | async-start | bytes 131072 | tf_op jit(solution)/shard_map/all_to_all | solution.py:40
  146.5 13.9 %while.37 = (s32[]{:T(128)}, f32[1,8,8]{2,1,0:T(8,128)S(1)}, f32[1,8,8,128]{3,2,1,0:T(8,128)S(1)}, f32[1,8,8]{2,1,0:T(8,128)S(1)}, s32[1]{0:T(128)}, /*index=5*/...) while((s32[]{:T(128)}, f32[1,8,8]{2,1,0:T(8,128)S(1)}, ...), condition=%wide.region_13.14_spmd.clone, body=%wide.region_10.13_spmd.clone.sunk | while | flops 17098120 | bytes 2578623 | solution.py:108
  146.5 1.7 fusion.151
  148.2 1.6 fusion.153
  150.0 1.7 fusion.151
  151.7 1.6 fusion.153
  153.5 1.7 fusion.151
  155.2 1.6 fusion.153
  157.0 1.7 fusion.151
  158.7 1.6 fusion.153
  160.7 0.8 fusion.116
  161.6 0.7 copy.65
  162.2 0.7 fusion.85
  163.6 10.3 %all-to-all-start.2 = ((bf16[1,64,130]{2,0,1:T(2,128)(2,1)}), bf16[1,64,130]{2,0,1:T(2,128)(2,1)S(1)}, u32[]{:S(2)}, u32[]{:S(2)}) async-start(bf16[1,64,130]{2,0,1:T(2,128)(2,1)} %copy.65), calls=%async_computation.2 | async-start | bytes 131072 | tf_op jit(solution)/shard_map/all_to_all | solution.py:40
  173.9 0.7 slice_reduce_fusion.1
  175.3 1.0 fusion.70
  177.0 0.2 fusion.69
  177.2 1.0 fusion.42
  178.2 5.8 %all-to-all-done.2 = bf16[1,64,130]{2,0,1:T(2,128)(2,1)S(1)} async-done(((bf16[1,64,130]{2,0,1:T(2,128)(2,1)}), bf16[1,64,130]{2,0,1:T(2,128)(2,1)S(1)}, u32[]{:S(2)}, u32[]{:S(2)}) %all-to-all-start.2) | async-done | bytes 16672 | tf_op jit(solution)/shard_map/all_to_all | solution.py:40
  184.0 4.5 %all-to-all-start.1 = ((f32[64,128,1]{1,2,0:T(1,128)}), f32[64,128,1]{1,2,0:T(1,128)S(1)}, u32[]{:S(2)}, u32[]{:S(2)}) async-start(f32[64,128,1]{1,2,0:T(1,128)} %fusion.42), calls=%async_computation.1 | async-start | bytes 65536 | tf_op jit(solution)/shard_map/all_to_all | solution.py:53
  188.5 0.7 slice_reduce_fusion
  190.4 0.6 fusion.111
  191.0 1.0 fusion.72
  193.3 0.2 fusion.71
  193.5 1.1 fusion.45
  194.6 3.3 %all-to-all-done.1 = f32[64,128,1]{1,2,0:T(1,128)S(1)} async-done(((f32[64,128,1]{1,2,0:T(1,128)}), f32[64,128,1]{1,2,0:T(1,128)S(1)}, u32[]{:S(2)}, u32[]{:S(2)}) %all-to-all-start.1) | async-done | bytes 32800 | tf_op jit(solution)/shard_map/all_to_all | solution.py:53
  197.9 7.0 %all-to-all-start.3 = ((f32[64,128,1]{1,2,0:T(1,128)}), f32[64,128,1]{1,2,0:T(1,128)S(1)}, u32[]{:S(2)}, u32[]{:S(2)}) async-start(f32[64,128,1]{1,2,0:T(1,128)} %fusion.45), calls=%async_computation.3 | async-start | bytes 65536 | tf_op jit(solution)/shard_map/all_to_all | solution.py:53
  205.0 9.3 %all-to-all-done.3 = f32[64,128,1]{1,2,0:T(1,128)S(1)} async-done(((f32[64,128,1]{1,2,0:T(1,128)}), f32[64,128,1]{1,2,0:T(1,128)S(1)}, u32[]{:S(2)}, u32[]{:S(2)}) %all-to-all-start.3) | async-done | bytes 32800 | tf_op jit(solution)/shard_map/all_to_all | solution.py:53
  214.4 0.5 copy.69
  (147 shorter events, 5.1 us)
Async XLA Ops:
  0.0 177.2 %copy-start = (bf16[128,8192]{1,0:T(8,128)(2,1)S(1)}, bf16[128,8192]{1,0:T(8,128)(2,1)}, u32[]{:S(2)}) copy-start(bf16[128,8192]{1,0:T(8,128)(2,1)} %param.19) | copy-start | bytes 6291460
  3.1 7.1 %copy-start.1 = (bf16[8192,128]{1,0:T(8,128)(2,1)S(1)}, bf16[8192,128]{1,0:T(8,128)(2,1)}, u32[]{:S(2)}) copy-start(bf16[8192,128]{1,0:T(8,128)(2,1)} %param.16) | copy-start | bytes 6291460
  4.9 5.9 %copy-start.3 = (bf16[8192,16]{0,1:T(8,128)(2,1)S(1)}, bf16[8192,16]{0,1:T(8,128)(2,1)}, u32[]{:S(2)}) copy-start(bf16[8192,16]{0,1:T(8,128)(2,1)} %param.18) | copy-start | bytes 786436
  4.9 6.3 %copy-start.4 = (bf16[8192,16]{0,1:T(8,128)(2,1)S(1)}, bf16[8192,16]{0,1:T(8,128)(2,1)}, u32[]{:S(2)}) copy-start(bf16[8192,16]{0,1:T(8,128)(2,1)} %param.17) | copy-start | bytes 786436
  6.9 92.8 %collective-permute-start = (bf16[1,128]{1,0:T(2,128)(2,1)S(1)}, bf16[1,128]{1,0:T(2,128)(2,1)S(1)}, u32[]{:S(2)}, u32[]{:S(2)}) collective-permute-start(bf16[1,128]{1,0:T(2,128)(2,1)S(1)} %bitcast.334), channel_id=1, source_target_pairs={{0,4},{4,0},{8,12},{12,8},{16,20},{20,16},{24,28},{28,24},{32,36},... | collective-permute-start | bytes 776 | tf_op jit(solution)/shard_map/ppermute | solution.py:17
  10.7 90.1 %collective-permute-start.6 = (bf16[1,128]{1,0:T(2,128)(2,1)S(1)}, bf16[1,128]{1,0:T(2,128)(2,1)S(1)}, u32[]{:S(2)}, u32[]{:S(2)}) collective-permute-start(bf16[1,128]{1,0:T(2,128)(2,1)S(1)} %bitcast.332), channel_id=1, source_target_pairs={{0,4},{4,0},{8,12},{12,8},{16,20},{20,16},{24,28},{28,24},{32,36},... | collective-permute-start | bytes 776 | tf_op jit(solution)/shard_map/ppermute | solution.py:17
  91.8 4.8 %copy-start.2 = (bf16[1,2048,8,128]{3,2,1,0:T(8,128)(2,1)S(1)}, bf16[1,2048,8,128]{3,2,1,0:T(8,128)(2,1)}, u32[]{:S(2)}) copy-start(bf16[1,2048,8,128]{3,2,1,0:T(8,128)(2,1)} %param.21) | copy-start | bytes 12582916
  99.7 2.5 %collective-permute-start.1 = (bf16[1,256]{1,0:T(2,128)(2,1)S(1)}, bf16[1,256]{1,0:T(2,128)(2,1)S(1)}, u32[]{:S(2)}, u32[]{:S(2)}) collective-permute-start(bf16[1,256]{1,0:T(2,128)(2,1)S(1)} %broadcast_select_fusion.9), channel_id=1, source_target_pairs={{0,8},{4,12},{8,0},{12,4},{16,24},{20,28},{24,16},{28,20},{32,40},... | collective-permute-start | bytes 1544 | tf_op jit(solution)/shard_map/ppermute | solution.py:17
  100.7 3.3 %collective-permute-start.7 = (bf16[1,256]{1,0:T(2,128)(2,1)S(1)}, bf16[1,256]{1,0:T(2,128)(2,1)S(1)}, u32[]{:S(2)}, u32[]{:S(2)}) collective-permute-start(bf16[1,256]{1,0:T(2,128)(2,1)S(1)} %broadcast_select_fusion.8), channel_id=1, source_target_pairs={{0,8},{4,12},{8,0},{12,4},{16,24},{20,28},{24,16},{28,20},{32,40},... | collective-permute-start | bytes 1544 | tf_op jit(solution)/shard_map/ppermute | solution.py:17
  102.2 4.0 %collective-permute-start.2 = (bf16[1,512]{1,0:T(2,128)(2,1)S(1)}, bf16[1,512]{1,0:T(2,128)(2,1)S(1)}, u32[]{:S(2)}, u32[]{:S(2)}) collective-permute-start(bf16[1,512]{1,0:T(2,128)(2,1)S(1)} %broadcast_select_fusion.7), channel_id=1, source_target_pairs={{0,16},{4,20},{8,24},{12,28},{16,0},{20,4},{24,8},{28,12},{32,48},... | collective-permute-start | bytes 3080 | tf_op jit(solution)/shard_map/ppermute | solution.py:17
  104.0 4.3 %collective-permute-start.8 = (bf16[1,512]{1,0:T(2,128)(2,1)S(1)}, bf16[1,512]{1,0:T(2,128)(2,1)S(1)}, u32[]{:S(2)}, u32[]{:S(2)}) collective-permute-start(bf16[1,512]{1,0:T(2,128)(2,1)S(1)} %broadcast_select_fusion.6), channel_id=1, source_target_pairs={{0,16},{4,20},{8,24},{12,28},{16,0},{20,4},{24,8},{28,12},{32,48},... | collective-permute-start | bytes 3080 | tf_op jit(solution)/shard_map/ppermute | solution.py:17
  106.3 2.5 %collective-permute-start.3 = (bf16[1,1024]{1,0:T(2,128)(2,1)S(1)}, bf16[1,1024]{1,0:T(2,128)(2,1)S(1)}, u32[]{:S(2)}, u32[]{:S(2)}) collective-permute-start(bf16[1,1024]{1,0:T(2,128)(2,1)S(1)} %broadcast_select_fusion.5), channel_id=1, source_target_pairs={{0,32},{4,36},{8,40},{12,44},{16,48},{20,52},{24,56},{28,60},{32,0... | collective-permute-start | bytes 6152 | tf_op jit(solution)/shard_map/ppermute | solution.py:17
  108.4 2.5 %collective-permute-start.9 = (bf16[1,1024]{1,0:T(2,128)(2,1)S(1)}, bf16[1,1024]{1,0:T(2,128)(2,1)S(1)}, u32[]{:S(2)}, u32[]{:S(2)}) collective-permute-start(bf16[1,1024]{1,0:T(2,128)(2,1)S(1)} %broadcast_select_fusion.4), channel_id=1, source_target_pairs={{0,32},{4,36},{8,40},{12,44},{16,48},{20,52},{24,56},{28,60},{32,0... | collective-permute-start | bytes 6152 | tf_op jit(solution)/shard_map/ppermute | solution.py:17
  108.9 3.7 %collective-permute-start.4 = (bf16[1,2048]{1,0:T(2,128)(2,1)S(1)}, bf16[1,2048]{1,0:T(2,128)(2,1)S(1)}, u32[]{:S(2)}, u32[]{:S(2)}) collective-permute-start(bf16[1,2048]{1,0:T(2,128)(2,1)S(1)} %broadcast_select_fusion.3), channel_id=1, source_target_pairs={{0,64},{4,68},{8,72},{12,76},{16,80},{20,84},{24,88},{28,92},{32,9... | collective-permute-start | bytes 12296 | tf_op jit(solution)/shard_map/ppermute | solution.py:17
  110.9 4.8 %collective-permute-start.10 = (bf16[1,2048]{1,0:T(2,128)(2,1)S(1)}, bf16[1,2048]{1,0:T(2,128)(2,1)S(1)}, u32[]{:S(2)}, u32[]{:S(2)}) collective-permute-start(bf16[1,2048]{1,0:T(2,128)(2,1)S(1)} %broadcast_select_fusion.2), channel_id=1, source_target_pairs={{0,64},{4,68},{8,72},{12,76},{16,80},{20,84},{24,88},{28,92},{32,9... | collective-permute-start | bytes 12296 | tf_op jit(solution)/shard_map/ppermute | solution.py:17
  112.7 6.6 %collective-permute-start.5 = (bf16[1,4096]{1,0:T(2,128)(2,1)S(1)}, bf16[1,4096]{1,0:T(2,128)(2,1)S(1)}, u32[]{:S(2)}, u32[]{:S(2)}) collective-permute-start(bf16[1,4096]{1,0:T(2,128)(2,1)S(1)} %broadcast_select_fusion.1), channel_id=1, source_target_pairs={{0,128},{4,132},{8,136},{12,140},{16,144},{20,148},{24,152},{28,15... | collective-permute-start | bytes 24584 | tf_op jit(solution)/shard_map/ppermute | solution.py:17
  115.8 30.5 %collective-permute-start.11 = (bf16[1,4096]{1,0:T(2,128)(2,1)S(1)}, bf16[1,4096]{1,0:T(2,128)(2,1)S(1)}, u32[]{:S(2)}, u32[]{:S(2)}) collective-permute-start(bf16[1,4096]{1,0:T(2,128)(2,1)S(1)} %broadcast_select_fusion), channel_id=1, source_target_pairs={{0,128},{4,132},{8,136},{12,140},{16,144},{20,148},{24,152},{28,15... | collective-permute-start | bytes 24584 | tf_op jit(solution)/shard_map/ppermute | solution.py:17
  134.4 29.2 %all-to-all-start = ((bf16[1,64,130]{2,0,1:T(2,128)(2,1)}), bf16[1,64,130]{2,0,1:T(2,128)(2,1)S(1)}, u32[]{:S(2)}, u32[]{:S(2)}) async-start(bf16[1,64,130]{2,0,1:T(2,128)(2,1)} %copy.59), calls=%async_computation | async-start | bytes 131072 | tf_op jit(solution)/shard_map/all_to_all | solution.py:40
  163.6 20.4 %all-to-all-start.2 = ((bf16[1,64,130]{2,0,1:T(2,128)(2,1)}), bf16[1,64,130]{2,0,1:T(2,128)(2,1)S(1)}, u32[]{:S(2)}, u32[]{:S(2)}) async-start(bf16[1,64,130]{2,0,1:T(2,128)(2,1)} %copy.65), calls=%async_computation.2 | async-start | bytes 131072 | tf_op jit(solution)/shard_map/all_to_all | solution.py:40
  184.0 13.9 %all-to-all-start.1 = ((f32[64,128,1]{1,2,0:T(1,128)}), f32[64,128,1]{1,2,0:T(1,128)S(1)}, u32[]{:S(2)}, u32[]{:S(2)}) async-start(f32[64,128,1]{1,2,0:T(1,128)} %fusion.42), calls=%async_computation.1 | async-start | bytes 65536 | tf_op jit(solution)/shard_map/all_to_all | solution.py:53
  197.9 16.4 %all-to-all-start.3 = ((f32[64,128,1]{1,2,0:T(1,128)}), f32[64,128,1]{1,2,0:T(1,128)S(1)}, u32[]{:S(2)}, u32[]{:S(2)}) async-start(f32[64,128,1]{1,2,0:T(1,128)} %fusion.45), calls=%async_computation.3 | async-start | bytes 65536 | tf_op jit(solution)/shard_map/all_to_all | solution.py:53
